TPU v7x, 32 devices: a whole 2x2x4 slice. The times are simulated.
32 devices in a mesh: frame: 8 (over y, x, core), tensor: 4 (over z).
Axes of the slice: x: 2, y: 2, z: 4, core: 2. Of those that a mesh axis runs over, the one named last changes fastest.
Arguments:
- tokens: bfloat16 [1024, 1, 4096], P(('frame', 'tensor')), may hold values from -6 to 6
- norm_gain: float32 [4096], replicated, may hold values from 0.5 to 1.5
- query_weight: bfloat16 [4096, 4096], P(None, 'tensor'), may hold values from -0.09375 to 0.09375
- out_weight: bfloat16 [4096, 4096], P('tensor'), may hold values from -0.09375 to 0.09375
- cache_keys: bfloat16 [384, 1, 4096], P('frame', None, 'tensor'), may hold values from -420 to 420
- cache_values: bfloat16 [384, 1, 4096], P('frame', None, 'tensor'), may hold values from -18 to 18
- token_pos: int32 [1024, 1], P('frame'), may hold values from 0 to 383, as said below
- frame_pad: int32 [1], replicated, may hold values from 0 to 192
Outputs:
- mixed: bfloat16 [1024, 1, 4096], P(('frame', 'tensor'))
Inputs may be any that keep to these rules, and one draw needn't show every extreme that they name: `token_pos`: nondecreasing along each sequence; the last token of every sequence has 383.
All inputs are finite; a program needn't handle non-finite values.
Results may differ from a plain program's by a relative error of at most 0.018.
Values may be sent and summed in bfloat16 or wider, within the bound.
A program may use at most 64 MiB of HBM per device.

v0:
```python
import jax
import jax.numpy as jnp
from jax import lax
from jax.sharding import PartitionSpec as P

HEAD_DIM = 128


epsilon = 1e-06
masked_score = -1e30


def normalize(block_rows, norm_gain):
    hidden = block_rows.astype(jnp.float32)
    factor = lax.rsqrt(jnp.mean(hidden * hidden, axis=-1, keepdims=True) + epsilon)
    return (hidden * factor * norm_gain).astype(jnp.bfloat16)


def per_device(
    tokens, norm_gain, query_weight, out_weight, cache_keys, cache_values, token_pos, frame_pad
):
    head_cols = query_weight.shape[1]
    heads_here = head_cols // HEAD_DIM
    seq_count = tokens.shape[1]
    query_scale = HEAD_DIM ** (-0.5)
    normed = normalize(lax.all_gather(tokens, "tensor", axis=0, tiled=True), norm_gain)
    queries = (
        jnp.dot(normed, query_weight, preferred_element_type=jnp.float32) * query_scale
    ).astype(jnp.bfloat16)
    query_rows = queries.shape[0]
    query_heads = queries.reshape(query_rows, seq_count, heads_here, HEAD_DIM)
    all_frames = cache_keys.shape[0] * lax.axis_size("frame")
    valid_frames = all_frames - frame_pad
    start_max = jnp.full((query_rows, seq_count, heads_here), masked_score, jnp.float32)
    running_max = start_max
    key_piece = lax.all_gather(cache_keys, "frame", axis=0, tiled=True)
    value_piece = lax.all_gather(cache_values, "frame", axis=0, tiled=True)
    row_count = key_piece.shape[0]
    frame_index = jnp.arange(row_count, dtype=jnp.int32)
    visible = (frame_index[None, None, :] <= token_pos[:, :, None]) & (
        frame_index[None, None, :] < valid_frames[None, :, None]
    )
    key_heads = key_piece.reshape(row_count, seq_count, heads_here, HEAD_DIM)
    scores = jnp.einsum(
        "rshd,fshd->rshf", query_heads, key_heads, preferred_element_type=jnp.float32
    )
    visible = visible[:, :, None, :]
    scores, visible = (jnp.where(visible, scores, masked_score), visible)
    new_max = jnp.maximum(running_max, jnp.max(scores, axis=-1))
    weights = jnp.where(visible, jnp.exp(scores - new_max[..., None]), 0.0)
    running_sum = jnp.sum(weights, axis=-1)
    value_heads = value_piece.reshape(value_piece.shape[0], seq_count, heads_here, HEAD_DIM)
    accumulated = jnp.einsum(
        "rshf,fshd->rshd",
        weights.astype(jnp.bfloat16),
        value_heads,
        preferred_element_type=jnp.float32,
    )
    running_max, running_sum, accumulated = (new_max, running_sum, accumulated)
    attended = (
        (accumulated / running_sum[..., None])
        .astype(jnp.bfloat16)
        .reshape(query_rows, seq_count, head_cols)
    )
    return lax.psum_scatter(
        jnp.dot(attended, out_weight, preferred_element_type=jnp.float32).astype(jnp.bfloat16),
        "tensor",
        scatter_dimension=0,
        tiled=True,
    )


def solution(mesh):
    placed = (
        P(("frame", "tensor"), None, None),
        P(),
        P(None, "tensor"),
        P("tensor", None),
        P("frame", None, "tensor"),
        P("frame", None, "tensor"),
        P("frame", None),
        P(),
    )
    return jax.shard_map(
        per_device,
        mesh=mesh,
        in_specs=placed,
        out_specs=P(("frame", "tensor"), None, None),
        check_vma=False,
    )
```

profile of v0, /device:TPU:0, one launch (start us, length us, event | category | flops | bytes accessed | tf_op | source)
XLA Modules:
  0.0 84.1 jit_solution(8908072664769119444)
XLA Ops:
  6.5 0.0 copy-start
  6.5 0.0 all-gather.2.cloned.1.call-start
  6.5 0.7 all-gather.2.cloned.1.call-update
  7.3 0.0 reduce-scatter.2.cloned.1.call-start
  8.0 12.2 %all_gather.10 = bf16[384,1,1024]{2,0,1:T(8,128)(2,1)S(1)} all-gather(bf16[48,1,1024]{2,0,1:T(8,128)(2,1)} %param.12), channel_id=1, replica_groups=mesh['frame'=8,'tensor'=4] {'frame'}, dimensions={0}, use_global_device_ids=true | all-gather | bytes 884736 | tf_op jit(solution)/shard_map/all_gather | solution.py:36
  20.2 0.4 copy.15
  20.5 0.0 copy-done
  20.6 0.0 copy-start.1
  20.6 0.0 copy-start.2
  20.6 10.0 %all_gather.11 = bf16[384,1,1024]{2,0,1:T(8,128)(2,1)S(1)} all-gather(bf16[48,1,1024]{2,0,1:T(8,128)(2,1)S(1)} %copy-done), channel_id=1, replica_groups=mesh['frame'=8,'tensor'=4] {'frame'}, dimensions={0}, use_global_device_ids=true | all-gather | bytes 884736 | tf_op jit(solution)/shard_map/all_gather | solution.py:37
  30.6 0.4 copy.18
  31.0 0.0 copy-done.1
  31.0 0.1 fusion.21
  31.1 8.5 %all-gather.2.cloned.1.call-done = bf16[128,1,4096]{2,0,1:T(8,128)(2,1)} async-done(((bf16[32,1,4096]{2,0,1:T(8,128)(2,1)}), bf16[128,1,4096]{2,0,1:T(8,128)(2,1)}) %all-gather.2.cloned.1.call-update) | async-done | bytes 1048592 | tf_op jit(solution)/shard_map/all_gather | solution.py:26
  39.6 0.0 slice-start
  39.6 1.7 %fusion.1 = f32[128]{0:T(128)S(1)} fusion(bf16[128,1,4096]{2,0,1:T(8,128)(2,1)} %all-gather.2.cloned.1.call-done), kind=kLoop, calls=%fused_computation.4 | loop fusion | flops 1572736 | bytes 1049088 | tf_op jit(solution)/shard_map/reduce_sum | solution.py:15
  41.3 0.0 copy-done.2
  41.3 0.0 slice-start.1
  41.3 5.2 %fusion.7 = bf16[16,8,8,128]{3,2,1,0:T(8,128)(2,1)S(1)} fusion(bf16[4096,1024]{1,0:T(8,128)(2,1)} %param.10, bf16[128,1,4096]{2,0,1:T(8,128)(2,1)} %all-gather.2.cloned.1.call-done, f32[4096]{0:T(1024)S(1)} %copy-done.2, f32[128]{0:T(128)S(1)} %add_rsqrt_fusion), kind=kOutput, calls=%fused_computation.14 | convolution fusion | flops 1076101120 | bytes 9716224 | tf_op jit(solution)/shard_map/dot_general | solution.py:28
  46.5 0.5 fusion.23
  47.0 0.6 fusion.4
  47.6 0.6 fusion.13
  48.1 0.0 slice-done
  48.2 0.0 slice-done.1
  48.2 2.3 %fusion = bf16[128,1,4096]{2,0,1:T(8,128)(2,1)} fusion(bf16[128,1024]{0,1:T(8,128)(2,1)S(1)} %bitcast.45, bf16[1024,4096]{1,0:T(8,128)(2,1)S(1)} %bitcast.42), kind=kOutput, calls=%fused_computation.1 | convolution fusion | flops 1074266112 | bytes 9699328 | tf_op jit(solution)/shard_map/dot_general | solution.py:66
  50.4 0.0 reduce-scatter.2.cloned.1.call-update
  50.5 26.8 %reduce-scatter.2.cloned.1.call-done = bf16[32,1,4096]{2,0,1:T(8,128)(2,1)} async-done(((bf16[128,1,4096]{2,0,1:T(8,128)(2,1)}), bf16[32,1,4096]{2,0,1:T(8,128)(2,1)}) %reduce-scatter.2.cloned.1.call-update) | async-done | bytes 262160 | tf_op jit(solution)/shard_map/reduce_scatter | solution.py:65
  (4 shorter events, 0.0 us)
Async XLA Ops:
  6.5 14.0 %copy-start = (bf16[48,1,1024]{2,0,1:T(8,128)(2,1)S(1)}, bf16[48,1,1024]{2,0,1:T(8,128)(2,1)}, u32[]{:S(2)}) copy-start(bf16[48,1,1024]{2,0,1:T(8,128)(2,1)} %param.13) | copy-start | bytes 294916
  6.5 33.1 %all-gather.2.cloned.1.call-start = ((), (), s32[]{:S(2)}) async-start(), calls=%async_computation.1 | async-start | bytes 1310720 | tf_op jit(solution)/shard_map/all_gather | solution.py:26
  7.3 70.0 %reduce-scatter.2.cloned.1.call-start = ((), (), s32[]{:S(2)}) async-start(), calls=%async_computation.2 | async-start | bytes 1310720 | tf_op jit(solution)/shard_map/reduce_scatter | solution.py:65
  20.6 10.4 %copy-start.1 = (s32[128,1]{0,1:T(1,128)S(1)}, s32[128,1]{0,1:T(1,128)}, u32[]{:S(2)}) copy-start(s32[128,1]{0,1:T(1,128)} %param.14) | copy-start | bytes 1540
  20.6 20.8 %copy-start.2 = (f32[4096]{0:T(1024)S(1)}, f32[4096]{0:T(1024)}, u32[]{:S(2)}) copy-start(f32[4096]{0:T(1024)} %param.9) | copy-start | bytes 49156
  39.6 8.5 %slice-start = ((s8[8388608]{0:T(1024)(128)(4,1)}), s8[4194304]{0:T(1024)(128)(4,1)S(1)}, s32[]{:S(2)}) async-start(s8[8388608]{0:T(1024)(128)(4,1)} %bitcast.41), calls=%async_computation.3 | async-start | bytes 8388608
  41.3 6.8 %slice-start.1 = ((s8[8388608]{0:T(1024)(128)(4,1)}), s8[4194304]{0:T(1024)(128)(4,1)S(1)}, s32[]{:S(2)}) async-start(s8[8388608]{0:T(1024)(128)(4,1)} %bitcast.41), calls=%async_computation.4 | async-start | bytes 8388608
Sparse Core Ops, SparseCore 0:
  8.9 30.6 all-gather.1
  50.6 26.6 reduce-scatter.1
where the time goes:
time: 84.3 us; the launch traced here: 84.1 us
  waiting for transfers between devices  36.1 us (43%)
  blocking collectives  22.3 us (26%)
  between operations  14.2 us (17%)
  matrix products  8.47 us (10%)
  other arithmetic  2.36 us (3%)
    reduce_scatter x1, waiting for transfers between devices, per_device(): lax.psum_scatter(jnp.dot(attended, out_weight, preferred_element_type=jnp...  26.8 us
    all_gather x1, blocking collectives, per_device(): key_piece = lax.all_gather(cache_keys, 'frame', axis=0, tiled=True)  12.2 us
    all_gather x1, blocking collectives, per_device(): value_piece = lax.all_gather(cache_values, 'frame', axis=0, tiled=True)  10 us
    all_gather x1, waiting for transfers between devices, per_device(): lax.all_gather(tokens, 'tensor', axis=0, tiled=True)  8.55 us
    dot_general x1, matrix products, per_device(): jnp.dot(normed, query_weight, preferred_element_type=jnp.float32)  5.17 us
    dot_general x1, matrix products, per_device(): jnp.dot(attended, out_weight, preferred_element_type=jnp.float32)  2.26 us
  transfers between devices with their start and end apart: 2, of which 2 were waited for; matrix products, arithmetic and copies ran while one was open for 1% of the time, Pallas kernels for 0%

commit v1 on v0

v1 whole, which is shorter than its diff:
```python
import functools
import math

import jax
import jax.numpy as jnp
from jax import lax
from jax.experimental import pallas as pl
from jax.experimental.pallas import tpu as pltpu
from jax.sharding import PartitionSpec as P

HEAD_DIM = 128
epsilon = 1e-06
masked_score = -1e30
MESH = pl.DeviceIdType.MESH


def flip(index, bit):
    return index + bit - 2 * bit * lax.rem(lax.div(index, bit), 2)


def kernel(
    n, frames_n, q_tile, o_tile, parts,
    tok, gain, wq_hbm, wo_hbm, keys, values, pos, pad,
    out,
    wq, wo, kg, vg, xg, nbuf, qbuf, abuf, pbuf, rbuf,
    load_sem, own_sem, kv_own, k_send, k_recv, v_send, v_recv,
    x_send, x_recv, p_send, p_recv,
):
    me_f = lax.axis_index("frame")
    me = lax.axis_index("tensor")
    rows = tok.shape[0]
    width = tok.shape[1]
    cols = wq.shape[1]
    span = keys.shape[0]
    bits = [1 << b for b in range(int(math.log2(frames_n)))][::-1]
    k_order = bits
    v_order = bits[1::-1] + bits[2:] if len(bits) > 1 else bits
    n_out = width // o_tile

    def load(src, dst, slot, part):
        depth = dst.shape[0] // parts
        window = pl.ds(part * depth, depth)
        return pltpu.make_async_copy(src.at[window], dst.at[window], load_sem.at[slot, part])

    q_loads = [load(wq_hbm, wq, 0, i) for i in range(parts)]
    o_loads = [load(wo_hbm, wo, 1, i) for i in range(parts)]
    own_x = pltpu.make_async_copy(tok, xg.at[me], own_sem)
    own_k = pltpu.make_async_copy(keys, kg.at[pl.ds(0, span)], kv_own.at[0])
    own_v = pltpu.make_async_copy(values, vg.at[pl.ds(0, span)], kv_own.at[1])

    barrier = pltpu.get_barrier_semaphore()
    for step in range(1, n):
        pl.semaphore_signal(
            barrier, inc=1, device_id={"tensor": lax.rem(me + step, n)}, device_id_type=MESH
        )
    for bit in bits:
        pl.semaphore_signal(
            barrier, inc=1, device_id={"frame": flip(me_f, bit)}, device_id_type=MESH
        )
    own_x.start()
    own_k.start()
    own_v.start()
    for copy in q_loads + o_loads:
        copy.start()
    pl.semaphore_wait(barrier, n - 1 + len(bits))

    def token_copy(block, side, source=None):
        towards = me + 1 if side == 0 else me - 1
        towards = lax.rem(towards + n, n)
        return pltpu.make_async_remote_copy(
            src_ref=xg.at[block] if source is None else source,
            dst_ref=xg.at[block],
            send_sem=x_send.at[side, block],
            recv_sem=x_recv.at[block],
            device_id={"tensor": towards},
            device_id_type=MESH,
        )

    @pl.when(me < n - 1)
    def _():
        token_copy(me, 0, tok).start()

    @pl.when(me > 0)
    def _():
        token_copy(me, 1, tok).start()

    def exchange(ref, source, send, recv, order, phase):
        bit = order[phase]
        held = [0]
        for earlier in order[:phase]:
            held = held + [slot + earlier for slot in held]
        copies = []
        for slot in held:
            src = source if slot == 0 else ref.at[pl.ds(slot * span, span)]
            copies.append(
                pltpu.make_async_remote_copy(
                    src_ref=src,
                    dst_ref=ref.at[pl.ds((slot + bit) * span, span)],
                    send_sem=send.at[slot + bit],
                    recv_sem=recv.at[slot + bit],
                    device_id={"frame": flip(me_f, bit)},
                    device_id_type=MESH,
                )
            )
        return copies

    phases = [
        exchange(kg, keys, k_send, k_recv, k_order, p)
        + exchange(vg, values, v_send, v_recv, v_order, p)
        for p in range(len(bits))
    ]

    def begin(p):
        for copy in phases[p]:
            copy.start()

    def finish(p):
        for copy in phases[p]:
            copy.wait_recv()

    begin(0)
    for p in range(1, len(bits)):
        finish(p - 1)
        begin(p)

    slot_of = lax.broadcasted_iota(jnp.int32, (1, span), 1)
    pieces = []
    for slot in range(frames_n):
        owner = me_f
        for bit in bits:
            if slot & bit:
                owner = flip(owner, bit)
        pieces.append(slot_of + owner * span)
    frame_index = jnp.concatenate(pieces, axis=1)
    visible_frames = frame_index < frames_n * span - pad[0]

    def part_copy(block, tile, slot=None):
        window = pl.ds(pl.multiple_of(tile * o_tile, o_tile), o_tile)
        return pltpu.make_async_remote_copy(
            src_ref=pbuf.at[block, :, window],
            dst_ref=rbuf.at[me if slot is None else slot, :, window],
            send_sem=p_send.at[block, tile],
            recv_sem=p_recv.at[me if slot is None else slot, tile],
            device_id={"tensor": block},
            device_id_type=MESH,
        )

    def process(block, first, mine):
        hidden = xg[block].astype(jnp.float32)
        factor = lax.rsqrt(jnp.mean(hidden * hidden, axis=-1, keepdims=True) + epsilon)
        nbuf[...] = (hidden * factor * gain[...]).astype(jnp.bfloat16)

        @pl.when(first)
        def _():
            for copy in q_loads:
                copy.wait()

        def q_body(tile, _):
            window = pl.ds(pl.multiple_of(tile * q_tile, q_tile), q_tile)
            q = jnp.dot(nbuf[...], wq[:, window], preferred_element_type=jnp.float32)
            qbuf[:, window] = (q * HEAD_DIM ** (-0.5)).astype(jnp.bfloat16)
            return 0

        lax.fori_loop(0, cols // q_tile, q_body, 0)

        @pl.when(first)
        def _():
            finish(len(bits) - 1)
            own_k.wait()
            own_v.wait()

        block_pos = pos[pl.ds(pl.multiple_of(block * rows, rows), rows), :]
        visible = (frame_index <= block_pos) & visible_frames
        for head in range(cols // HEAD_DIM):
            window = slice(head * HEAD_DIM, (head + 1) * HEAD_DIM)
            scores = lax.dot_general(
                qbuf[:, window], kg[:, window], (((1,), (1,)), ((), ())),
                preferred_element_type=jnp.float32,
            )
            scores = jnp.where(visible, scores, masked_score)
            highest = jnp.max(scores, axis=-1, keepdims=True)
            weights = jnp.where(visible, jnp.exp(scores - highest), 0.0)
            total = jnp.sum(weights, axis=-1, keepdims=True)
            mixed = jnp.dot(
                weights.astype(jnp.bfloat16), vg[:, window], preferred_element_type=jnp.float32
            )
            abuf[:, window] = (mixed / total).astype(jnp.bfloat16)

        @pl.when(first)
        def _():
            for copy in o_loads:
                copy.wait()

        def o_body(tile, _):
            window = pl.ds(pl.multiple_of(tile * o_tile, o_tile), o_tile)
            pbuf[block, :, window] = jnp.dot(
                abuf[...], wo[:, window], preferred_element_type=jnp.float32
            ).astype(jnp.bfloat16)

            @pl.when(jnp.logical_and(jnp.logical_not(mine), tile > 0))
            def _():
                part_copy(block, tile - 1).start()

            return 0

        lax.fori_loop(0, n_out, o_body, 0)

        @pl.when(jnp.logical_not(mine))
        def _():
            part_copy(block, n_out - 1).start()

    def round_body(index, _):
        stage = lax.div(index, 2) + 1
        side = lax.rem(index, 2)
        before = me - stage
        after = me + stage

        @pl.when(jnp.logical_and(side == 0, before >= 0))
        def _():
            token_copy(before, 0).wait_recv()

            @pl.when(me < n - 1)
            def _():
                token_copy(before, 0).start()

        @pl.when(jnp.logical_and(side == 0, after < n))
        def _():
            token_copy(after, 1).wait_recv()

            @pl.when(me > 0)
            def _():
                token_copy(after, 1).start()

        mine = index == 2 * (n - 1)

        @pl.when(mine)
        def _():
            own_x.wait()

        block = jnp.where(mine, me, jnp.where(side == 0, before, after))
        first = jnp.logical_or(index == 0, jnp.logical_and(index == 1, me == 0))

        @pl.when(jnp.logical_and(block >= 0, block < n))
        def _():
            process(block, first, mine)

        return 0

    lax.fori_loop(0, 2 * (n - 1) + 1, round_body, 0)

    def sum_body(tile, _):
        window = pl.ds(pl.multiple_of(tile * o_tile, o_tile), o_tile)
        total = pbuf[me, :, window].astype(jnp.float32)
        for step in range(1, n):
            peer = lax.rem(me + step, n)
            part_copy(peer, tile, peer).wait_recv()
            total = total + rbuf[peer, :, window].astype(jnp.float32)
        out[:, window] = total.astype(jnp.bfloat16)
        return 0

    lax.fori_loop(0, n_out, sum_body, 0)

    def drain_body(step, _):
        peer = lax.rem(me + step, n)
        for tile in range(n_out):
            part_copy(peer, tile).wait_send()
        return 0

    lax.fori_loop(1, n, drain_body, 0)

    def drain_tokens(block, _):
        @pl.when(jnp.logical_and(me < n - 1, block <= me))
        def _():
            token_copy(block, 0).wait_send()

        @pl.when(jnp.logical_and(me > 0, block >= me))
        def _():
            token_copy(block, 1).wait_send()

        return 0

    lax.fori_loop(0, n, drain_tokens, 0)
    for group in phases:
        for copy in group:
            copy.wait_send()


def divisor(total, most):
    return math.gcd(total, most)


def per_device(
    n, frames_n,
    tokens, norm_gain, query_weight, out_weight, cache_keys, cache_values, token_pos, frame_pad
):
    rows, seqs, width = tokens.shape
    cols = query_weight.shape[1]
    span = cache_keys.shape[0]
    q_tile = divisor(cols, 512)
    o_tile = divisor(width, 1024)
    parts = 4
    n_out = width // o_tile
    hbm = pl.BlockSpec(memory_space=pl.ANY)
    vmem = pl.BlockSpec(memory_space=pltpu.VMEM)
    bf16 = jnp.bfloat16
    dma = pltpu.SemaphoreType.DMA
    result = pl.pallas_call(
        functools.partial(kernel, n, frames_n, q_tile, o_tile, parts),
        out_shape=jax.ShapeDtypeStruct((rows, width), bf16),
        in_specs=[hbm, vmem, hbm, hbm, hbm, hbm, vmem, pl.BlockSpec(memory_space=pltpu.SMEM)],
        out_specs=vmem,
        scratch_shapes=[
            pltpu.VMEM(query_weight.shape, bf16),
            pltpu.VMEM(out_weight.shape, bf16),
            pltpu.VMEM((frames_n * span, cols), bf16),
            pltpu.VMEM((frames_n * span, cols), bf16),
            pltpu.VMEM((n, rows, width), bf16),
            pltpu.VMEM((rows, width), bf16),
            pltpu.VMEM((rows, cols), bf16),
            pltpu.VMEM((rows, cols), bf16),
            pltpu.VMEM((n, rows, width), bf16),
            pltpu.VMEM((n, rows, width), bf16),
            dma((2, parts)),
            dma(()),
            dma((2,)),
            dma((frames_n,)),
            dma((frames_n,)),
            dma((frames_n,)),
            dma((frames_n,)),
            dma((2, n)),
            dma((n,)),
            dma((n, n_out)),
            dma((n, n_out)),
        ],
        compiler_params=pltpu.CompilerParams(collective_id=0, has_side_effects=True),
    )(
        tokens.reshape(rows, width),
        norm_gain.reshape(1, width),
        query_weight,
        out_weight,
        cache_keys.reshape(span, cols),
        cache_values.reshape(span, cols),
        token_pos,
        frame_pad,
    )
    return result.reshape(rows, seqs, width)


def solution(mesh):
    placed = (
        P(("frame", "tensor"), None, None),
        P(),
        P(None, "tensor"),
        P("tensor", None),
        P("frame", None, "tensor"),
        P("frame", None, "tensor"),
        P("frame", None),
        P(),
    )
    return jax.shard_map(
        functools.partial(per_device, mesh.shape["tensor"], mesh.shape["frame"]),
        mesh=mesh,
        in_specs=placed,
        out_specs=P(("frame", "tensor"), None, None),
        check_vma=False,
    )
```

time: 84.3 us -> 58.2 us (0.69)
  Pallas kernels: 0 us -> 54.2 us
  waiting for transfers between devices: 36.1 us -> 0 us
  blocking collectives: 22.3 us -> 0 us
  between operations: 14.2 us -> 0.66 us
  matrix products: 8.47 us -> 0 us
  other arithmetic: 2.36 us -> 0 us
  local copies, waits for them, and re-layouts: 0.73 us -> 3.06 us
    pallas_call x0 -> x1, Pallas kernels: none -> 54.2 us  [per_device(): pl.pallas_call(functools.partial(kernel, n, frames_n, q_tile, o_tile, par...]
    reduce_scatter x1 -> x0, waiting for transfers between devices: 26.8 us -> none  [per_device(): lax.psum_scatter(jnp.dot(attended, out_weight, preferred_element_type=jnp...]
    all_gather x2 -> x0, blocking collectives: 22.3 us -> none  [the longest x1 12.2 us: per_device(): key_piece = lax.all_gather(cache_keys, 'frame', axis=0, tiled=True)]
    all_gather x1 -> x0, waiting for transfers between devices: 8.55 us -> none  [per_device(): lax.all_gather(tokens, 'tensor', axis=0, tiled=True)]
    dot_general x4 -> x0, matrix products: 8.47 us -> none  [the longest x1 5.17 us: per_device(): jnp.dot(normed, query_weight, preferred_element_type=jnp.float32)]
    unnamed x10 -> x2, local copies, waits for them, and re-layouts: 0.03 us -> 3.06 us
    reduce_sum x2 -> x0, other arithmetic: 2.24 us -> none  [the longest x1 1.67 us: normalize(): jnp.mean(hidden * hidden, axis=-1, keepdims=True) + epsilon]
  transfers between devices with their start and end apart: 2 -> 0, of which waited for: 2 -> 0; matrix products, arithmetic and copies ran while one was open for 1% -> 0% of each run, Pallas kernels for 0% -> 0%
where the time goes in v1:
time: 58.2 us; the launch traced here: 57.9 us
  Pallas kernels  54.2 us (93%)
  local copies, waits for them, and re-layouts  3.06 us (5%)
  between operations  0.66 us (1%)
    pallas_call x1, Pallas kernels, per_device(): pl.pallas_call(functools.partial(kernel, n, frames_n, q_tile, o_tile, par...  54.2 us
    unnamed x2, local copies, waits for them, and re-layouts  3.06 us

profile of v1, /device:TPU:0, one launch (start us, length us, event | category | flops | bytes accessed | tf_op | source)
XLA Modules:
  0.0 57.9 jit_solution(17778175005162505974)
XLA Ops:
  0.7 1.4 %copy.9.pos = s32[128,1]{1,0:T(8,128)} copy(s32[128,1]{0,1:T(1,128)} %param.14) | data formatting | bytes 1024 | tf_op args[6]
  2.0 54.2 %shard_map.82 = bf16[32,4096]{1,0:T(8,128)(2,1)} custom-call(bf16[32,4096]{1,0:T(8,128)(2,1)} %bitcast.6, f32[1,4096]{1,0:T(1,128)} %bitcast.9, bf16[4096,1024]{1,0:T(8,128)(2,1)} %wq_hbm.1, bf16[1024,4096]{1,0:T(8,128)(2,1)} %wo_hbm.1, bf16[48,1024]{1,0:T(8,128)(2,1)} %bitcast.7, bf16[48,1024]{1,0:T(8,128)(2,1)} %bitcast.8, s32[128,1]{1,0:T(8,128)} %copy.9.pos, ...), custom_call_target="tpu_custom_call" | custom-call | tf_op jit(solution)/shard_map/pallas_call | solution.py:307
  56.3 1.7 %copy.12 = bf16[32,1,4096]{2,0,1:T(8,128)(2,1)} copy(bf16[32,1,4096]{2,0,1:T(8,128)(2,1)} %bitcast.5) | data formatting | bytes 524288

commit v2 on v1

v2 whole, which is shorter than its diff:
```python
import functools
import math

import jax
import jax.numpy as jnp
from jax import lax
from jax.experimental import pallas as pl
from jax.experimental.pallas import tpu as pltpu
from jax.sharding import PartitionSpec as P

HEAD_DIM = 128
epsilon = 1e-06
masked_score = -1e30
MESH = pl.DeviceIdType.MESH


def flip(index, bit):
    return index + bit - 2 * bit * lax.rem(lax.div(index, bit), 2)


def kernel(
    n, frames_n, x_tile, o_tile,
    tok, gain, wq_hbm, wo_hbm, keys, values, pos, pad,
    out,
    wq, wo, kg, vg, raw, xg, qacc, qall, abuf, pbuf, rbuf,
    q_sem, o_sem, own_sem, kv_own, k_send, k_recv, v_send, v_recv,
    x_send, x_recv, p_send, p_recv,
):
    me_f = lax.axis_index("frame")
    me = lax.axis_index("tensor")
    rows = tok.shape[0]
    width = tok.shape[1]
    cols = wq.shape[1]
    span = keys.shape[0]
    bits = [1 << b for b in range(int(math.log2(frames_n)))][::-1]
    phase_n = len(bits)
    v_order = bits[1::-1] + bits[2:] if phase_n > 1 else bits
    n_x = width // x_tile
    n_out = width // o_tile
    has_left = me > 0
    has_right = me < n - 1
    middle = jnp.logical_and(has_left, has_right)
    low_half = 2 * me < n

    def q_load(part):
        window = pl.ds(pl.multiple_of(part * x_tile, x_tile), x_tile)
        return pltpu.make_async_copy(wq_hbm.at[window], wq.at[window], q_sem.at[part])

    def o_load(part):
        depth = cols // 2
        window = pl.ds(part * depth, depth)
        return pltpu.make_async_copy(wo_hbm.at[window], wo.at[window], o_sem.at[part])

    own_x = pltpu.make_async_copy(tok, raw, own_sem)
    own_k = pltpu.make_async_copy(keys, kg.at[pl.ds(0, span)], kv_own.at[0])
    own_v = pltpu.make_async_copy(values, vg.at[pl.ds(0, span)], kv_own.at[1])

    own_x.start()
    barrier = pltpu.get_barrier_semaphore()
    for bit in bits:
        pl.semaphore_signal(
            barrier, inc=1, device_id={"frame": flip(me_f, bit)}, device_id_type=MESH
        )

    @pl.when(has_left)
    def _():
        pl.semaphore_signal(barrier, inc=1, device_id={"tensor": me - 1}, device_id_type=MESH)

    @pl.when(has_right)
    def _():
        pl.semaphore_signal(barrier, inc=1, device_id={"tensor": me + 1}, device_id_type=MESH)

    own_k.start()
    own_v.start()
    for part in range(n_x):
        q_load(part).start()
    for part in range(2):
        o_load(part).start()

    own_x.wait()
    hidden = raw[...].astype(jnp.float32)
    factor = lax.rsqrt(jnp.mean(hidden * hidden, axis=-1, keepdims=True) + epsilon)
    xg[me] = (hidden * factor * gain[...]).astype(jnp.bfloat16)

    pl.semaphore_wait(barrier, phase_n + jnp.minimum(me, 1) + jnp.minimum(n - 1 - me, 1))

    def token_copy(block, side, chunk):
        towards = lax.rem(me + 1 - 2 * side + n, n)
        window = pl.ds(pl.multiple_of(chunk * x_tile, x_tile), x_tile)
        return pltpu.make_async_remote_copy(
            src_ref=xg.at[block, :, window],
            dst_ref=xg.at[block, :, window],
            send_sem=x_send.at[side, block, chunk],
            recv_sem=x_recv.at[block, chunk],
            device_id={"tensor": towards},
            device_id_type=MESH,
        )

    for chunk in range(n_x):
        @pl.when(has_right)
        def _():
            token_copy(me, 0, chunk).start()

        @pl.when(has_left)
        def _():
            token_copy(me, 1, chunk).start()

    def exchange(ref, source, send, recv, order, phase):
        bit = order[phase]
        held = [0]
        for earlier in order[:phase]:
            held = held + [slot + earlier for slot in held]
        copies = []
        for slot in held:
            src = source if slot == 0 else ref.at[pl.ds(slot * span, span)]
            copies.append(
                pltpu.make_async_remote_copy(
                    src_ref=src,
                    dst_ref=ref.at[pl.ds((slot + bit) * span, span)],
                    send_sem=send.at[slot + bit],
                    recv_sem=recv.at[slot + bit],
                    device_id={"frame": flip(me_f, bit)},
                    device_id_type=MESH,
                )
            )
        return copies

    phases = [
        exchange(kg, keys, k_send, k_recv, bits, p)
        + exchange(vg, values, v_send, v_recv, v_order, p)
        for p in range(phase_n)
    ]

    def begin(p):
        for copy in phases[p]:
            copy.start()

    def finish(p):
        for copy in phases[p]:
            copy.wait_recv()

    begin(0)

    slot_of = lax.broadcasted_iota(jnp.int32, (1, span), 1)
    pieces = []
    for slot in range(frames_n):
        owner = me_f
        for bit in bits:
            if slot & bit:
                owner = flip(owner, bit)
        pieces.append(slot_of + owner * span)
    frame_index = jnp.concatenate(pieces, axis=1)
    visible_frames = frame_index < frames_n * span - pad[0]

    def q_step(block, side, chunk):
        window = pl.ds(pl.multiple_of(chunk * x_tile, x_tile), x_tile)
        product = jnp.dot(xg[block, :, window], wq[window, :], preferred_element_type=jnp.float32)

        @pl.when(chunk == 0)
        def _():
            qacc[side] = product

        @pl.when(chunk > 0)
        def _():
            qacc[side] += product

        @pl.when(chunk == n_x - 1)
        def _():
            qall[block] = (qacc[side] * HEAD_DIM ** (-0.5)).astype(jnp.bfloat16)

    def own_body(chunk, _):
        q_load(chunk).wait()
        q_step(me, 0, chunk)
        return 0

    lax.fori_loop(0, n_x, own_body, 0)
    for p in range(1, phase_n - 1):
        finish(p - 1)
        begin(p)

    def part_copy(block, side, tile):
        towards = lax.rem(me + 1 - 2 * side + n, n)
        window = pl.ds(pl.multiple_of(tile * o_tile, o_tile), o_tile)
        return pltpu.make_async_remote_copy(
            src_ref=pbuf.at[block, :, window],
            dst_ref=rbuf.at[side, block, :, window],
            send_sem=p_send.at[block, tile],
            recv_sem=p_recv.at[side, block, tile],
            device_id={"tensor": towards},
            device_id_type=MESH,
        )

    def attend(block, send, side):
        block_pos = pos[pl.ds(pl.multiple_of(block * rows, rows), rows), :]
        visible = (frame_index <= block_pos) & visible_frames
        for head in range(cols // HEAD_DIM):
            window = slice(head * HEAD_DIM, (head + 1) * HEAD_DIM)
            scores = lax.dot_general(
                qall[block, :, window], kg[:, window], (((1,), (1,)), ((), ())),
                preferred_element_type=jnp.float32,
            )
            scores = jnp.where(visible, scores, masked_score)
            highest = jnp.max(scores, axis=-1, keepdims=True)
            weights = jnp.where(visible, jnp.exp(scores - highest), 0.0)
            total = jnp.sum(weights, axis=-1, keepdims=True)
            mixed = jnp.dot(
                weights.astype(jnp.bfloat16), vg[:, window], preferred_element_type=jnp.float32
            )
            abuf[:, window] = (mixed / total).astype(jnp.bfloat16)

        def o_body(tile, _):
            window = pl.ds(pl.multiple_of(tile * o_tile, o_tile), o_tile)
            pbuf[block, :, window] = jnp.dot(
                abuf[...], wo[:, window], preferred_element_type=jnp.float32
            ).astype(jnp.bfloat16)
            if send:
                @pl.when(tile > 0)
                def _():
                    part_copy(block, side, tile - 1).start()
            return 0

        lax.fori_loop(0, n_out, o_body, 0)
        if send:
            part_copy(block, side, n_out - 1).start()

    def stage_body(stage, _):
        before = me - stage
        after = me + stage

        def chunk_body(chunk, _):
            @pl.when(before >= 0)
            def _():
                token_copy(before, 0, chunk).wait_recv()

                @pl.when(has_right)
                def _():
                    token_copy(before, 0, chunk).start()

            @pl.when(after < n)
            def _():
                token_copy(after, 1, chunk).wait_recv()

                @pl.when(has_left)
                def _():
                    token_copy(after, 1, chunk).start()

            def side_body(side, _):
                block = me + (2 * side - 1) * stage

                @pl.when(jnp.logical_and(block >= 0, block < n))
                def _():
                    q_step(block, side, chunk)

                return 0

            lax.fori_loop(0, 2, side_body, 0)
            return 0

        lax.fori_loop(0, n_x, chunk_body, 0)

        @pl.when(stage == 1)
        def _():
            if phase_n > 1:
                finish(phase_n - 2)
                begin(phase_n - 1)
            finish(phase_n - 1)
            own_k.wait()
            own_v.wait()
            for part in range(2):
                o_load(part).wait()

        @pl.when(jnp.logical_not(middle))
        def _():
            attend(
                jnp.where(has_left, n - 1 - stage, stage), True, jnp.where(has_left, 1, 0)
            )

        return 0

    lax.fori_loop(1, n, stage_body, 0)

    def late_body(index, _):
        step = jnp.where(low_half, index, n - index)
        block = lax.rem(me + step, n)

        @pl.when(jnp.logical_or(middle, index == n))
        def _():
            attend(block, False, 0)

        return 0

    lax.fori_loop(1, n + 1, late_body, 0)

    def relay_body(index, _):
        stage = lax.div(index, n_out)
        tile = lax.rem(index, n_out)
        window = pl.ds(pl.multiple_of(tile * o_tile, o_tile), o_tile)

        def side_body(turn, _):
            side = jnp.where(low_half, turn, 1 - turn)
            block = jnp.where(side == 0, stage, n - 1 - stage)
            passes = jnp.where(side == 0, block > me, block < me)

            @pl.when(jnp.logical_and(middle, passes))
            def _():
                part_copy(block, side, tile).wait_recv()
                pbuf[block, :, window] = (
                    pbuf[block, :, window].astype(jnp.float32)
                    + rbuf[side, block, :, window].astype(jnp.float32)
                ).astype(jnp.bfloat16)
                part_copy(block, side, tile).start()

            return 0

        lax.fori_loop(0, 2, side_body, 0)
        return 0

    lax.fori_loop(n_out, n * n_out, relay_body, 0)

    def sum_body(tile, _):
        window = pl.ds(pl.multiple_of(tile * o_tile, o_tile), o_tile)

        @pl.when(has_left)
        def _():
            part_copy(me, 0, tile).wait_recv()

        @pl.when(has_right)
        def _():
            part_copy(me, 1, tile).wait_recv()

        total = pbuf[me, :, window].astype(jnp.float32)
        zero = jnp.zeros_like(total)
        total = total + jnp.where(has_left, rbuf[0, me, :, window].astype(jnp.float32), zero)
        total = total + jnp.where(has_right, rbuf[1, me, :, window].astype(jnp.float32), zero)
        out[:, window] = total.astype(jnp.bfloat16)
        return 0

    lax.fori_loop(0, n_out, sum_body, 0)

    def drain_body(block, _):
        for tile in range(n_out):
            @pl.when(block != me)
            def _():
                part_copy(block, 0, tile).wait_send()

        for chunk in range(n_x):
            @pl.when(jnp.logical_and(has_right, block <= me))
            def _():
                token_copy(block, 0, chunk).wait_send()

            @pl.when(jnp.logical_and(has_left, block >= me))
            def _():
                token_copy(block, 1, chunk).wait_send()

        return 0

    lax.fori_loop(0, n, drain_body, 0)
    for group in phases:
        for copy in group:
            copy.wait_send()


def divisor(total, most):
    return math.gcd(total, most)


def per_device(
    n, frames_n,
    tokens, norm_gain, query_weight, out_weight, cache_keys, cache_values, token_pos, frame_pad
):
    rows, seqs, width = tokens.shape
    cols = query_weight.shape[1]
    span = cache_keys.shape[0]
    x_tile = divisor(width, 1024)
    o_tile = divisor(width, 1024)
    n_x = width // x_tile
    n_out = width // o_tile
    hbm = pl.BlockSpec(memory_space=pl.ANY)
    vmem = pl.BlockSpec(memory_space=pltpu.VMEM)
    bf16 = jnp.bfloat16
    dma = pltpu.SemaphoreType.DMA
    result = pl.pallas_call(
        functools.partial(kernel, n, frames_n, x_tile, o_tile),
        out_shape=jax.ShapeDtypeStruct((rows, width), bf16),
        in_specs=[hbm, vmem, hbm, hbm, hbm, hbm, vmem, pl.BlockSpec(memory_space=pltpu.SMEM)],
        out_specs=vmem,
        scratch_shapes=[
            pltpu.VMEM(query_weight.shape, bf16),
            pltpu.VMEM(out_weight.shape, bf16),
            pltpu.VMEM((frames_n * span, cols), bf16),
            pltpu.VMEM((frames_n * span, cols), bf16),
            pltpu.VMEM((rows, width), bf16),
            pltpu.VMEM((n, rows, width), bf16),
            pltpu.VMEM((2, rows, cols), jnp.float32),
            pltpu.VMEM((n, rows, cols), bf16),
            pltpu.VMEM((rows, cols), bf16),
            pltpu.VMEM((n, rows, width), bf16),
            pltpu.VMEM((2, n, rows, width), bf16),
            dma((n_x,)),
            dma((2,)),
            dma(()),
            dma((2,)),
            dma((frames_n,)),
            dma((frames_n,)),
            dma((frames_n,)),
            dma((frames_n,)),
            dma((2, n, n_x)),
            dma((n, n_x)),
            dma((n, n_out)),
            dma((2, n, n_out)),
        ],
        compiler_params=pltpu.CompilerParams(collective_id=0, has_side_effects=True),
    )(
        tokens.reshape(rows, width),
        norm_gain.reshape(1, width),
        query_weight,
        out_weight,
        cache_keys.reshape(span, cols),
        cache_values.reshape(span, cols),
        token_pos,
        frame_pad,
    )
    return result.reshape(rows, seqs, width)


def solution(mesh):
    placed = (
        P(("frame", "tensor"), None, None),
        P(),
        P(None, "tensor"),
        P("tensor", None),
        P("frame", None, "tensor"),
        P("frame", None, "tensor"),
        P("frame", None),
        P(),
    )
    return jax.shard_map(
        functools.partial(per_device, mesh.shape["tensor"], mesh.shape["frame"]),
        mesh=mesh,
        in_specs=placed,
        out_specs=P(("frame", "tensor"), None, None),
        check_vma=False,
    )
```

time: 58.2 us -> 62.8 us (1.079)
  Pallas kernels: 54.2 us -> 58.8 us
    pallas_call x1, Pallas kernels: 54.2 us -> 58.8 us  [per_device(): pl.pallas_call(functools.partial(kernel, n, frames_n, x_tile, o_tile), ou...]
where the time goes in v2:
time: 62.8 us; the launch traced here: 62.5 us
  Pallas kernels  58.8 us (94%)
  local copies, waits for them, and re-layouts  3.06 us (5%)
  between operations  0.66 us (1%)
    pallas_call x1, Pallas kernels, per_device(): pl.pallas_call(functools.partial(kernel, n, frames_n, x_tile, o_tile), ou...  58.8 us
    unnamed x2, local copies, waits for them, and re-layouts  3.06 us

profile of v2, /device:TPU:0, one launch (start us, length us, event | category | flops | bytes accessed | tf_op | source)
XLA Modules:
  0.0 62.5 jit_solution(7782679189686264522)
XLA Ops:
  0.7 1.4 %copy.9.pos = s32[128,1]{1,0:T(8,128)} copy(s32[128,1]{0,1:T(1,128)} %param.14) | data formatting | bytes 1024 | tf_op args[6]
  2.0 58.8 %shard_map.82 = bf16[32,4096]{1,0:T(8,128)(2,1)} custom-call(bf16[32,4096]{1,0:T(8,128)(2,1)} %bitcast.6, f32[1,4096]{1,0:T(1,128)} %bitcast.9, bf16[4096,1024]{1,0:T(8,128)(2,1)} %wq_hbm.1, bf16[1024,4096]{1,0:T(8,128)(2,1)} %wo_hbm.1, bf16[48,1024]{1,0:T(8,128)(2,1)} %bitcast.7, bf16[48,1024]{1,0:T(8,128)(2,1)} %bitcast.8, s32[128,1]{1,0:T(8,128)} %copy.9.pos, ...), custom_call_target="tpu_custom_call" | custom-call | tf_op jit(solution)/shard_map/pallas_call | solution.py:382
  60.9 1.7 %copy.12 = bf16[32,1,4096]{2,0,1:T(8,128)(2,1)} copy(bf16[32,1,4096]{2,0,1:T(8,128)(2,1)} %bitcast.5) | data formatting | bytes 524288

commit v3 on v2

--- a/solution.py
+++ b/solution.py
@@ -37,6 +37,7 @@
     v_order = bits[1::-1] + bits[2:] if phase_n > 1 else bits
     n_x = width // x_tile
     n_out = width // o_tile
+    lag = n_out // 2
     has_left = me > 0
     has_right = me < n - 1
     middle = jnp.logical_and(has_left, has_right)
@@ -193,35 +194,43 @@
     def attend(block, send, side):
         block_pos = pos[pl.ds(pl.multiple_of(block * rows, rows), rows), :]
         visible = (frame_index <= block_pos) & visible_frames
-        for head in range(cols // HEAD_DIM):
-            window = slice(head * HEAD_DIM, (head + 1) * HEAD_DIM)
-            scores = lax.dot_general(
+        windows = [slice(i, i + HEAD_DIM) for i in range(0, cols, HEAD_DIM)]
+        scores = [
+            lax.dot_general(
                 qall[block, :, window], kg[:, window], (((1,), (1,)), ((), ())),
                 preferred_element_type=jnp.float32,
             )
-            scores = jnp.where(visible, scores, masked_score)
-            highest = jnp.max(scores, axis=-1, keepdims=True)
-            weights = jnp.where(visible, jnp.exp(scores - highest), 0.0)
-            total = jnp.sum(weights, axis=-1, keepdims=True)
-            mixed = jnp.dot(
-                weights.astype(jnp.bfloat16), vg[:, window], preferred_element_type=jnp.float32
-            )
-            abuf[:, window] = (mixed / total).astype(jnp.bfloat16)
+            for window in windows
+        ]
+        scores = [jnp.where(visible, score, masked_score) for score in scores]
+        highest = [jnp.max(score, axis=-1, keepdims=True) for score in scores]
+        weights = [
+            jnp.where(visible, jnp.exp(score - top), 0.0) for score, top in zip(scores, highest)
+        ]
+        totals = [jnp.sum(weight, axis=-1, keepdims=True) for weight in weights]
+        gathered = [
+            jnp.dot(weight.astype(jnp.bfloat16), vg[:, window], preferred_element_type=jnp.float32)
+            for weight, window in zip(weights, windows)
+        ]
+        for window, value, total in zip(windows, gathered, totals):
+            abuf[:, window] = (value / total).astype(jnp.bfloat16)
 
         def o_body(tile, _):
             window = pl.ds(pl.multiple_of(tile * o_tile, o_tile), o_tile)
             pbuf[block, :, window] = jnp.dot(
                 abuf[...], wo[:, window], preferred_element_type=jnp.float32
             ).astype(jnp.bfloat16)
-            if send:
-                @pl.when(tile > 0)
+            if send is not False:
+                @pl.when(jnp.logical_and(send, tile > 0))
                 def _():
                     part_copy(block, side, tile - 1).start()
             return 0
 
         lax.fori_loop(0, n_out, o_body, 0)
-        if send:
-            part_copy(block, side, n_out - 1).start()
+        if send is not False:
+            @pl.when(send)
+            def _():
+                part_copy(block, side, n_out - 1).start()
 
     def stage_body(stage, _):
         before = me - stage
@@ -269,39 +278,32 @@
             for part in range(2):
                 o_load(part).wait()
 
-        @pl.when(jnp.logical_not(middle))
-        def _():
+        @pl.when(jnp.logical_or(jnp.logical_not(middle), stage == 1))
+        def _():
+            end_block = jnp.where(has_left, n - 1 - stage, stage)
+            near_block = jnp.where(low_half, me + 1, me - 1)
             attend(
-                jnp.where(has_left, n - 1 - stage, stage), True, jnp.where(has_left, 1, 0)
+                jnp.where(middle, near_block, end_block),
+                jnp.logical_not(middle),
+                jnp.where(has_left, 1, 0),
             )
 
         return 0
 
     lax.fori_loop(1, n, stage_body, 0)
 
-    def late_body(index, _):
-        step = jnp.where(low_half, index, n - index)
-        block = lax.rem(me + step, n)
-
-        @pl.when(jnp.logical_or(middle, index == n))
-        def _():
-            attend(block, False, 0)
-
-        return 0
-
-    lax.fori_loop(1, n + 1, late_body, 0)
-
     def relay_body(index, _):
-        stage = lax.div(index, n_out)
-        tile = lax.rem(index, n_out)
-        window = pl.ds(pl.multiple_of(tile * o_tile, o_tile), o_tile)
-
         def side_body(turn, _):
             side = jnp.where(low_half, turn, 1 - turn)
+            at = index - turn * lag
+            stage = lax.div(at, n_out)
+            tile = lax.rem(at, n_out)
+            window = pl.ds(pl.multiple_of(tile * o_tile, o_tile), o_tile)
             block = jnp.where(side == 0, stage, n - 1 - stage)
             passes = jnp.where(side == 0, block > me, block < me)
-
-            @pl.when(jnp.logical_and(middle, passes))
+            known = jnp.logical_and(at >= n_out, at < n * n_out)
+
+            @pl.when(jnp.logical_and(known, passes))
             def _():
                 part_copy(block, side, tile).wait_recv()
                 pbuf[block, :, window] = (
@@ -315,7 +317,21 @@
         lax.fori_loop(0, 2, side_body, 0)
         return 0
 
-    lax.fori_loop(n_out, n * n_out, relay_body, 0)
+    def late_body(index, _):
+        step = jnp.where(low_half, index, n - index)
+        block = lax.rem(me + step, n)
+
+        @pl.when(jnp.logical_and(middle, index == n))
+        def _():
+            lax.fori_loop(n_out, n * n_out + lag, relay_body, 0)
+
+        @pl.when(jnp.logical_or(middle, index == n))
+        def _():
+            attend(block, False, 0)
+
+        return 0
+
+    lax.fori_loop(2, n + 1, late_body, 0)
 
     def sum_body(tile, _):
         window = pl.ds(pl.multiple_of(tile * o_tile, o_tile), o_tile)
@@ -372,7 +388,7 @@
     cols = query_weight.shape[1]
     span = cache_keys.shape[0]
     x_tile = divisor(width, 1024)
-    o_tile = divisor(width, 1024)
+    o_tile = divisor(width, 512)
     n_x = width // x_tile
     n_out = width // o_tile
     hbm = pl.BlockSpec(memory_space=pl.ANY)

time: 62.8 us -> 49.8 us (0.79)
  Pallas kernels: 58.8 us -> 45.8 us
    pallas_call x1, Pallas kernels: 58.8 us -> 45.8 us  [per_device(): pl.pallas_call(functools.partial(kernel, n, frames_n, x_tile, o_tile), ou...]
where the time goes in v3:
time: 49.8 us; the launch traced here: 49.6 us
  Pallas kernels  45.8 us (92%)
  local copies, waits for them, and re-layouts  3.06 us (6%)
  between operations  0.66 us (1%)
    pallas_call x1, Pallas kernels, per_device(): pl.pallas_call(functools.partial(kernel, n, frames_n, x_tile, o_tile), ou...  45.8 us
    unnamed x2, local copies, waits for them, and re-layouts  3.06 us

profile of v3, /device:TPU:0, one launch (start us, length us, event | category | flops | bytes accessed | tf_op | source)
XLA Modules:
  0.0 49.6 jit_solution(7417484212431336670)
XLA Ops:
  0.7 1.4 %copy.9.pos = s32[128,1]{1,0:T(8,128)} copy(s32[128,1]{0,1:T(1,128)} %param.14) | data formatting | bytes 1024 | tf_op args[6]
  2.0 45.8 %shard_map.82 = bf16[32,4096]{1,0:T(8,128)(2,1)} custom-call(bf16[32,4096]{1,0:T(8,128)(2,1)} %bitcast.6, f32[1,4096]{1,0:T(1,128)} %bitcast.9, bf16[4096,1024]{1,0:T(8,128)(2,1)} %wq_hbm.1, bf16[1024,4096]{1,0:T(8,128)(2,1)} %wo_hbm.1, bf16[48,1024]{1,0:T(8,128)(2,1)} %bitcast.7, bf16[48,1024]{1,0:T(8,128)(2,1)} %bitcast.8, s32[128,1]{1,0:T(8,128)} %copy.9.pos, ...), custom_call_target="tpu_custom_call" | custom-call | tf_op jit(solution)/shard_map/pallas_call | solution.py:398
  47.9 1.7 %copy.12 = bf16[32,1,4096]{2,0,1:T(8,128)(2,1)} copy(bf16[32,1,4096]{2,0,1:T(8,128)(2,1)} %bitcast.5) | data formatting | bytes 524288

commit v4 on v3

--- a/solution.py
+++ b/solution.py
@@ -71,6 +71,12 @@
     def _():
         pl.semaphore_signal(barrier, inc=1, device_id={"tensor": me + 1}, device_id_type=MESH)
 
+    @pl.when(jnp.logical_not(middle))
+    def _():
+        pl.semaphore_signal(
+            barrier, inc=1, device_id={"tensor": n - 1 - me}, device_id_type=MESH
+        )
+
     own_k.start()
     own_v.start()
     for part in range(n_x):
@@ -83,7 +89,7 @@
     factor = lax.rsqrt(jnp.mean(hidden * hidden, axis=-1, keepdims=True) + epsilon)
     xg[me] = (hidden * factor * gain[...]).astype(jnp.bfloat16)
 
-    pl.semaphore_wait(barrier, phase_n + jnp.minimum(me, 1) + jnp.minimum(n - 1 - me, 1))
+    pl.semaphore_wait(barrier, phase_n + 2)
 
     def token_copy(block, side, chunk):
         towards = lax.rem(me + 1 - 2 * side + n, n)
@@ -179,19 +185,20 @@
         finish(p - 1)
         begin(p)
 
-    def part_copy(block, side, tile):
-        towards = lax.rem(me + 1 - 2 * side + n, n)
+    def part_copy(block, side, tile, far=False):
+        towards = jnp.where(far, block, lax.rem(me + 1 - 2 * side + n, n))
+        slot = jnp.where(far, 1 - side, side)
         window = pl.ds(pl.multiple_of(tile * o_tile, o_tile), o_tile)
         return pltpu.make_async_remote_copy(
             src_ref=pbuf.at[block, :, window],
-            dst_ref=rbuf.at[side, block, :, window],
+            dst_ref=rbuf.at[slot, block, :, window],
             send_sem=p_send.at[block, tile],
-            recv_sem=p_recv.at[side, block, tile],
+            recv_sem=p_recv.at[slot, block, tile],
             device_id={"tensor": towards},
             device_id_type=MESH,
         )
 
-    def attend(block, send, side):
+    def attend(block, send, side, far):
         block_pos = pos[pl.ds(pl.multiple_of(block * rows, rows), rows), :]
         visible = (frame_index <= block_pos) & visible_frames
         windows = [slice(i, i + HEAD_DIM) for i in range(0, cols, HEAD_DIM)]
@@ -220,17 +227,16 @@
             pbuf[block, :, window] = jnp.dot(
                 abuf[...], wo[:, window], preferred_element_type=jnp.float32
             ).astype(jnp.bfloat16)
-            if send is not False:
-                @pl.when(jnp.logical_and(send, tile > 0))
-                def _():
-                    part_copy(block, side, tile - 1).start()
+            @pl.when(jnp.logical_and(send, tile > 0))
+            def _():
+                part_copy(block, side, tile - 1, far).start()
+
             return 0
 
         lax.fori_loop(0, n_out, o_body, 0)
-        if send is not False:
-            @pl.when(send)
-            def _():
-                part_copy(block, side, n_out - 1).start()
+        @pl.when(send)
+        def _():
+            part_copy(block, side, n_out - 1, far).start()
 
     def stage_body(stage, _):
         before = me - stage
@@ -282,13 +288,18 @@
         def _():
             end_block = jnp.where(has_left, n - 1 - stage, stage)
             near_block = jnp.where(low_half, me + 1, me - 1)
-            attend(
-                jnp.where(middle, near_block, end_block),
-                jnp.logical_not(middle),
-                jnp.where(has_left, 1, 0),
-            )
-
-        return 0
+            block = jnp.where(middle, near_block, end_block)
+            ends = jnp.logical_not(middle)
+            send = jnp.logical_or(ends, starts_sum(block))
+            far = jnp.logical_and(ends, stage == n - 1)
+            attend(block, send, jnp.where(block > me, 0, 1), far)
+
+        return 0
+
+    def starts_sum(block):
+        up = jnp.logical_and(me == 1, block == n - 1)
+        down = jnp.logical_and(me == n - 2, block == 0)
+        return jnp.logical_or(up, down)
 
     lax.fori_loop(1, n, stage_body, 0)
 
@@ -296,12 +307,15 @@
         def side_body(turn, _):
             side = jnp.where(low_half, turn, 1 - turn)
             at = index - turn * lag
+            known = jnp.logical_and(at >= 0, at < (n - 1) * n_out)
+            at = jnp.maximum(at, 0)
             stage = lax.div(at, n_out)
+            stage = jnp.where(stage == 0, n - 1, stage)
             tile = lax.rem(at, n_out)
             window = pl.ds(pl.multiple_of(tile * o_tile, o_tile), o_tile)
             block = jnp.where(side == 0, stage, n - 1 - stage)
             passes = jnp.where(side == 0, block > me, block < me)
-            known = jnp.logical_and(at >= n_out, at < n * n_out)
+            passes = jnp.logical_and(passes, jnp.logical_not(starts_sum(block)))
 
             @pl.when(jnp.logical_and(known, passes))
             def _():
@@ -323,11 +337,12 @@
 
         @pl.when(jnp.logical_and(middle, index == n))
         def _():
-            lax.fori_loop(n_out, n * n_out + lag, relay_body, 0)
+            lax.fori_loop(0, (n - 1) * n_out + lag, relay_body, 0)
 
         @pl.when(jnp.logical_or(middle, index == n))
         def _():
-            attend(block, False, 0)
+            send = jnp.logical_and(middle, starts_sum(block))
+            attend(block, send, jnp.where(block > me, 0, 1), False)
 
         return 0
 
@@ -336,18 +351,10 @@
     def sum_body(tile, _):
         window = pl.ds(pl.multiple_of(tile * o_tile, o_tile), o_tile)
 
-        @pl.when(has_left)
-        def _():
-            part_copy(me, 0, tile).wait_recv()
-
-        @pl.when(has_right)
-        def _():
-            part_copy(me, 1, tile).wait_recv()
-
         total = pbuf[me, :, window].astype(jnp.float32)
-        zero = jnp.zeros_like(total)
-        total = total + jnp.where(has_left, rbuf[0, me, :, window].astype(jnp.float32), zero)
-        total = total + jnp.where(has_right, rbuf[1, me, :, window].astype(jnp.float32), zero)
+        for side in range(2):
+            part_copy(me, side, tile).wait_recv()
+            total = total + rbuf[side, me, :, window].astype(jnp.float32)
         out[:, window] = total.astype(jnp.bfloat16)
         return 0
 
@@ -388,7 +395,7 @@
     cols = query_weight.shape[1]
     span = cache_keys.shape[0]
     x_tile = divisor(width, 1024)
-    o_tile = divisor(width, 512)
+    o_tile = divisor(width, 1024)
     n_x = width // x_tile
     n_out = width // o_tile
     hbm = pl.BlockSpec(memory_space=pl.ANY)

time: 49.8 us -> 48 us (0.964)
  the two profiles are of different devices: /device:TPU:0 before, /device:TPU:11 now
where the time goes in v4:
time: 48 us; the launch traced here: 47.8 us
  Pallas kernels  44.1 us (92%)
  local copies, waits for them, and re-layouts  3.06 us (6%)
  between operations  0.66 us (1%)
    pallas_call x1, Pallas kernels, per_device(): pl.pallas_call(functools.partial(kernel, n, frames_n, x_tile, o_tile), ou...  44.1 us
    unnamed x2, local copies, waits for them, and re-layouts  3.06 us

profile of v4, /device:TPU:11, one launch (start us, length us, event | category | flops | bytes accessed | tf_op | source)
XLA Modules:
  0.0 47.8 jit_solution(17766451495350370998)
XLA Ops:
  0.7 1.4 %copy.9.pos = s32[128,1]{1,0:T(8,128)} copy(s32[128,1]{0,1:T(1,128)} %param.14) | data formatting | bytes 1024 | tf_op args[6]
  2.0 44.1 %shard_map.82 = bf16[32,4096]{1,0:T(8,128)(2,1)} custom-call(bf16[32,4096]{1,0:T(8,128)(2,1)} %bitcast.6, f32[1,4096]{1,0:T(1,128)} %bitcast.9, bf16[4096,1024]{1,0:T(8,128)(2,1)} %wq_hbm.1, bf16[1024,4096]{1,0:T(8,128)(2,1)} %wo_hbm.1, bf16[48,1024]{1,0:T(8,128)(2,1)} %bitcast.7, bf16[48,1024]{1,0:T(8,128)(2,1)} %bitcast.8, s32[128,1]{1,0:T(8,128)} %copy.9.pos, ...), custom_call_target="tpu_custom_call" | custom-call | tf_op jit(solution)/shard_map/pallas_call | solution.py:405
  46.1 1.7 %copy.12 = bf16[32,1,4096]{2,0,1:T(8,128)(2,1)} copy(bf16[32,1,4096]{2,0,1:T(8,128)(2,1)} %bitcast.5) | data formatting | bytes 524288

commit v5 on v4

--- a/solution.py
+++ b/solution.py
@@ -22,7 +22,7 @@
     n, frames_n, x_tile, o_tile,
     tok, gain, wq_hbm, wo_hbm, keys, values, pos, pad,
     out,
-    wq, wo, kg, vg, raw, xg, qacc, qall, abuf, pbuf, rbuf,
+    wq, wo, kg, vg, pos_col, raw, xg, qacc, qall, abuf, pbuf, rbuf, sums,
     q_sem, o_sem, own_sem, kv_own, k_send, k_recv, v_send, v_recv,
     x_send, x_recv, p_send, p_recv,
 ):
@@ -38,6 +38,7 @@
     n_x = width // x_tile
     n_out = width // o_tile
     lag = n_out // 2
+    passed = n_out // 2
     has_left = me > 0
     has_right = me < n - 1
     middle = jnp.logical_and(has_left, has_right)
@@ -84,6 +85,7 @@
     for part in range(2):
         o_load(part).start()
 
+    pos_col[...] = jnp.broadcast_to(pos[...], (HEAD_DIM, n * rows)).T
     own_x.wait()
     hidden = raw[...].astype(jnp.float32)
     factor = lax.rsqrt(jnp.mean(hidden * hidden, axis=-1, keepdims=True) + epsilon)
@@ -198,8 +200,16 @@
             device_id_type=MESH,
         )
 
+    def send_part(block, side, tile, far):
+        early = tile < passed
+        held = jnp.logical_and(middle, early)
+
+        @pl.when(jnp.logical_not(held))
+        def _():
+            part_copy(block, side, tile, jnp.logical_and(far, jnp.logical_not(early))).start()
+
     def attend(block, send, side, far):
-        block_pos = pos[pl.ds(pl.multiple_of(block * rows, rows), rows), :]
+        block_pos = pos_col[pl.ds(pl.multiple_of(block * rows, rows), rows), :1]
         visible = (frame_index <= block_pos) & visible_frames
         windows = [slice(i, i + HEAD_DIM) for i in range(0, cols, HEAD_DIM)]
         scores = [
@@ -229,14 +239,14 @@
             ).astype(jnp.bfloat16)
             @pl.when(jnp.logical_and(send, tile > 0))
             def _():
-                part_copy(block, side, tile - 1, far).start()
+                send_part(block, side, tile - 1, far)
 
             return 0
 
         lax.fori_loop(0, n_out, o_body, 0)
         @pl.when(send)
         def _():
-            part_copy(block, side, n_out - 1, far).start()
+            send_part(block, side, n_out - 1, far)
 
     def stage_body(stage, _):
         before = me - stage
@@ -307,15 +317,18 @@
         def side_body(turn, _):
             side = jnp.where(low_half, turn, 1 - turn)
             at = index - turn * lag
-            known = jnp.logical_and(at >= 0, at < (n - 1) * n_out)
+            known = jnp.logical_and(at >= 0, at < n * n_out)
             at = jnp.maximum(at, 0)
             stage = lax.div(at, n_out)
+            tile = lax.rem(at, n_out)
+            known = jnp.logical_and(known, jnp.logical_or(stage > 0, tile >= passed))
+            known = jnp.logical_and(known, jnp.logical_or(stage < n - 1, tile < passed))
             stage = jnp.where(stage == 0, n - 1, stage)
-            tile = lax.rem(at, n_out)
             window = pl.ds(pl.multiple_of(tile * o_tile, o_tile), o_tile)
             block = jnp.where(side == 0, stage, n - 1 - stage)
             passes = jnp.where(side == 0, block > me, block < me)
-            passes = jnp.logical_and(passes, jnp.logical_not(starts_sum(block)))
+            sent = jnp.logical_and(starts_sum(block), tile >= passed)
+            passes = jnp.logical_and(passes, jnp.logical_not(sent))
 
             @pl.when(jnp.logical_and(known, passes))
             def _():
@@ -337,7 +350,7 @@
 
         @pl.when(jnp.logical_and(middle, index == n))
         def _():
-            lax.fori_loop(0, (n - 1) * n_out + lag, relay_body, 0)
+            lax.fori_loop(0, n * n_out + lag, relay_body, 0)
 
         @pl.when(jnp.logical_or(middle, index == n))
         def _():
@@ -351,11 +364,17 @@
     def sum_body(tile, _):
         window = pl.ds(pl.multiple_of(tile * o_tile, o_tile), o_tile)
 
-        total = pbuf[me, :, window].astype(jnp.float32)
+        sums[...] = pbuf[me, :, window].astype(jnp.float32)
         for side in range(2):
-            part_copy(me, side, tile).wait_recv()
-            total = total + rbuf[side, me, :, window].astype(jnp.float32)
-        out[:, window] = total.astype(jnp.bfloat16)
+            from_far = jnp.logical_not(has_right if side else has_left)
+            comes = jnp.logical_not(jnp.logical_and(from_far, tile < passed))
+
+            @pl.when(comes)
+            def _():
+                part_copy(me, side, tile).wait_recv()
+                sums[...] += rbuf[side, me, :, window].astype(jnp.float32)
+
+        out[:, window] = sums[...].astype(jnp.bfloat16)
         return 0
 
     lax.fori_loop(0, n_out, sum_body, 0)
@@ -412,6 +431,7 @@
             pltpu.VMEM(out_weight.shape, bf16),
             pltpu.VMEM((frames_n * span, cols), bf16),
             pltpu.VMEM((frames_n * span, cols), bf16),
+            pltpu.VMEM((n * rows, HEAD_DIM), jnp.int32),
             pltpu.VMEM((rows, width), bf16),
             pltpu.VMEM((n, rows, width), bf16),
             pltpu.VMEM((2, rows, cols), jnp.float32),
@@ -419,6 +439,7 @@
             pltpu.VMEM((rows, cols), bf16),
             pltpu.VMEM((n, rows, width), bf16),
             pltpu.VMEM((2, n, rows, width), bf16),
+            pltpu.VMEM((rows, o_tile), jnp.float32),
             dma((n_x,)),
             dma((2,)),
             dma(()),
@@ -440,7 +461,7 @@
         out_weight,
         cache_keys.reshape(span, cols),
         cache_values.reshape(span, cols),
-        token_pos,
+        token_pos.reshape(1, n * rows),
         frame_pad,
     )
     return result.reshape(rows, seqs, width)

time: 48 us -> 49.4 us (1.029)
  the two profiles are of different devices: /device:TPU:11 before, /device:TPU:0 now
where the time goes in v5:
time: 49.4 us; the launch traced here: 49.1 us
  Pallas kernels  46.8 us (95%)
  local copies, waits for them, and re-layouts  1.67 us (3%)
  between operations  0.66 us (1%)
    pallas_call x1, Pallas kernels, per_device(): pl.pallas_call(functools.partial(kernel, n, frames_n, x_tile, o_tile), ou...  46.8 us
    unnamed x1, local copies, waits for them, and re-layouts  1.67 us

profile of v5, /device:TPU:0, one launch (start us, length us, event | category | flops | bytes accessed | tf_op | source)
XLA Modules:
  0.0 49.1 jit_solution(17808635990595927311)
XLA Ops:
  0.7 46.8 %shard_map.82 = bf16[32,4096]{1,0:T(8,128)(2,1)} custom-call(bf16[32,4096]{1,0:T(8,128)(2,1)} %bitcast.7, f32[1,4096]{1,0:T(1,128)} %bitcast.10, bf16[4096,1024]{1,0:T(8,128)(2,1)} %wq_hbm.1, bf16[1024,4096]{1,0:T(8,128)(2,1)} %wo_hbm.1, bf16[48,1024]{1,0:T(8,128)(2,1)} %bitcast.8, bf16[48,1024]{1,0:T(8,128)(2,1)} %bitcast.9, s32[1,128]{1,0:T(1,128)} %bitcast.11, ...), custom_call_target="tpu_custom_call" | custom-call | tf_op jit(solution)/shard_map/pallas_call | solution.py:424
  47.5 1.7 %copy.11 = bf16[32,1,4096]{2,0,1:T(8,128)(2,1)} copy(bf16[32,1,4096]{2,0,1:T(8,128)(2,1)} %bitcast.6) | data formatting | bytes 524288

commit v6 on v5

--- a/solution.py
+++ b/solution.py
@@ -38,7 +38,7 @@
     n_x = width // x_tile
     n_out = width // o_tile
     lag = n_out // 2
-    passed = n_out // 2
+    passed = 0
     has_left = me > 0
     has_right = me < n - 1
     middle = jnp.logical_and(has_left, has_right)

time: 49.4 us -> 46.5 us (0.941)
  the two profiles are of different devices: /device:TPU:0 before, /device:TPU:11 now
where the time goes in v6:
time: 46.5 us; the launch traced here: 46.3 us
  Pallas kernels  44 us (95%)
  local copies, waits for them, and re-layouts  1.67 us (4%)
  between operations  0.66 us (1%)
    pallas_call x1, Pallas kernels, per_device(): pl.pallas_call(functools.partial(kernel, n, frames_n, x_tile, o_tile), ou...  44 us
    unnamed x1, local copies, waits for them, and re-layouts  1.67 us

profile of v6, /device:TPU:11, one launch (start us, length us, event | category | flops | bytes accessed | tf_op | source)
XLA Modules:
  0.0 46.3 jit_solution(10006673152968413801)
XLA Ops:
  0.7 44.0 %shard_map.82 = bf16[32,4096]{1,0:T(8,128)(2,1)} custom-call(bf16[32,4096]{1,0:T(8,128)(2,1)} %bitcast.7, f32[1,4096]{1,0:T(1,128)} %bitcast.10, bf16[4096,1024]{1,0:T(8,128)(2,1)} %wq_hbm.1, bf16[1024,4096]{1,0:T(8,128)(2,1)} %wo_hbm.1, bf16[48,1024]{1,0:T(8,128)(2,1)} %bitcast.8, bf16[48,1024]{1,0:T(8,128)(2,1)} %bitcast.9, s32[1,128]{1,0:T(1,128)} %bitcast.11, ...), custom_call_target="tpu_custom_call" | custom-call | tf_op jit(solution)/shard_map/pallas_call | solution.py:424
  44.6 1.7 %copy.11 = bf16[32,1,4096]{2,0,1:T(8,128)(2,1)} copy(bf16[32,1,4096]{2,0,1:T(8,128)(2,1)} %bitcast.6) | data formatting | bytes 524288
